TPU v7x, 512 devices: a whole 4x4x16 slice. The times are simulated.
512 devices in a mesh: dp: 8 (over y, core), ctx: 64 (over z, x).
Axes of the slice: x: 4, y: 4, z: 16, core: 2. Of those that a mesh axis runs over, the one named last changes fastest.
Arguments:
- query_in: bfloat16 [8, 8192, 1792], P('dp', 'ctx'), may hold values from -8 to 8
- key_in: bfloat16 [8, 8192, 256], P('dp', 'ctx'), may hold values from -4 to 4
- value_input: bfloat16 [8, 8192, 256], P('dp', 'ctx'), may hold values from -4 to 4
- output_gradient: bfloat16 [8, 8192, 1792], P('dp', 'ctx'), may hold values from -5 to 5
- doc_ids: int32 [8, 8192], P('dp', 'ctx'), may hold values from 0 to 1, as said below
- query_bias: float32 [1792], replicated, may hold values from -2 to 2
Outputs:
- attended: bfloat16 [8, 8192, 1792], P('dp', 'ctx')
- grad_query: bfloat16 [8, 8192, 1792], P('dp', 'ctx')
- key_gradient: bfloat16 [8, 8192, 256], P('dp', 'ctx')
- value_gradient: bfloat16 [8, 8192, 256], P('dp', 'ctx')
- grad_bias: float32 [1792], replicated
Inputs may be any that keep to these rules, and one draw needn't show every extreme that they name: `doc_ids`: ids never fall along a sequence; each of the 2 documents of a sequence holds 2048 to 6144 tokens, and together they fill all 8192 tokens.
All inputs are finite; a program needn't handle non-finite values.
Results may differ from a plain program's by a relative error of at most 0.019.
Values may be sent and summed in bfloat16 or wider, within the bound.
A program may use at most 64 MiB of HBM per device.

v0:
```python
import math
import jax
import jax.numpy as jnp
from jax import lax
from jax.sharding import PartitionSpec as P

QUERY_HEADS = 14
KEY_VALUE_HEADS = 2
HEAD_SIZE = 128
GROUP_SIZE = 7
BLK = 128
WB = 16


def passed_along(value, axis, steps):
    count = lax.axis_size(axis)
    first, last = (max(0, -steps), min(count, count - steps))
    return lax.ppermute(value, axis, [(source, source + steps) for source in range(first, last)])


def split_pack(packed_block):
    head_size_width = KEY_VALUE_HEADS * HEAD_SIZE
    key_head_rows = packed_block[:, :head_size_width].reshape(
        packed_block.shape[0], KEY_VALUE_HEADS, HEAD_SIZE
    )
    value_head_rows = packed_block[:, head_size_width:].reshape(
        packed_block.shape[0], KEY_VALUE_HEADS, HEAD_SIZE
    )
    return (key_head_rows, value_head_rows)


def local(query_in, key_in, value_input, output_gradient, doc_ids, query_bias):
    sharded_rows = query_in.shape[1]
    ctx_count = lax.axis_size("ctx")
    ctx_rank = lax.axis_index("ctx")
    score_scale = 1.0 / math.sqrt(HEAD_SIZE)
    blocks_here = sharded_rows // BLK
    window_slots = min((WB - 1 + blocks_here - 1) // blocks_here, ctx_count - 1) + 1
    group_slots = max(1, min(window_slots, 512 // sharded_rows))
    group_count = -(-window_slots // group_slots)
    padded_slots = group_count * group_slots
    grouped_rows = group_slots * sharded_rows
    packed_width = 2 * KEY_VALUE_HEADS * HEAD_SIZE
    query_rows = (query_in[0].astype(jnp.float32) + query_bias).astype(jnp.bfloat16)
    query_head_rows = query_rows.reshape(sharded_rows, KEY_VALUE_HEADS, GROUP_SIZE, HEAD_SIZE)
    gradient_heads = output_gradient[0].reshape(
        sharded_rows, KEY_VALUE_HEADS, GROUP_SIZE, HEAD_SIZE
    )
    own_pack = jnp.concatenate([key_in[0], value_input[0]], axis=1)
    own_docs = doc_ids[0]
    query_pos = ctx_rank * sharded_rows + jnp.arange(sharded_rows, dtype=jnp.int32)
    first_pack = jnp.concatenate(
        [own_pack[None], jnp.zeros((window_slots - 1, sharded_rows, packed_width), jnp.bfloat16)],
        axis=0,
    )
    first_docs = jnp.concatenate(
        [own_docs[None], jnp.zeros((window_slots - 1, sharded_rows), jnp.int32)], axis=0
    )

    def pass_on(step_index, running):
        stored_pack, stored_docs, moving_pack, moving_docs = running
        moving_pack, moving_docs = passed_along((moving_pack, moving_docs), "ctx", 1)
        stored_pack = lax.dynamic_update_index_in_dim(stored_pack, moving_pack, step_index, 0)
        stored_docs = lax.dynamic_update_index_in_dim(stored_docs, moving_docs, step_index, 0)
        return (stored_pack, stored_docs, moving_pack, moving_docs)

    window_pack, window_docs, _, _ = lax.fori_loop(
        1, window_slots, pass_on, (first_pack, first_docs, own_pack, own_docs)
    )
    spare_slots = padded_slots - window_slots
    window_pack = jnp.concatenate(
        [window_pack, jnp.zeros((spare_slots, sharded_rows, packed_width), jnp.bfloat16)], axis=0
    )
    window_pack = window_pack.reshape(group_count, grouped_rows, packed_width)
    window_docs = jnp.concatenate(
        [window_docs, jnp.zeros((spare_slots, sharded_rows), jnp.int32)], axis=0
    )
    window_docs = window_docs.reshape(group_count, grouped_rows)
    group_ids = jnp.arange(group_count, dtype=jnp.int32)

    def group_mask(group_index, docs_block):
        key_index = jnp.arange(grouped_rows, dtype=jnp.int32)
        slot_index = group_index * group_slots + key_index // sharded_rows
        key_pos = (ctx_rank - slot_index) * sharded_rows + key_index % sharded_rows
        inside = ((slot_index < window_slots) & (key_pos >= 0))[None, :]
        causal = key_pos[None, :] <= query_pos[:, None]
        near = query_pos[:, None] // BLK - key_pos[None, :] // BLK < WB
        same_doc = own_docs[:, None] == docs_block[None, :]
        return inside & causal & near & same_doc

    def group_scores(packed_block, allowed):
        key_head_rows, value_head_rows = split_pack(packed_block)
        scores = (
            jnp.einsum(
                "qgnd,kgd->gnqk", query_head_rows, key_head_rows, preferred_element_type=jnp.float32
            )
            * score_scale
        )
        return (jnp.where(allowed[None, None], scores, -jnp.inf), key_head_rows, value_head_rows)

    def forward_work(running, packed_block, allowed):
        row_max, row_sum, weighted = running
        scores, key_head_rows, value_head_rows = group_scores(packed_block, allowed)
        new_max = jnp.maximum(row_max, jnp.max(scores, axis=-1))
        rescale = jnp.exp(row_max - new_max)
        weights = jnp.exp(scores - new_max[..., None])
        row_sum = row_sum * rescale + jnp.sum(weights, axis=-1)
        weighted = weighted * rescale[..., None] + jnp.einsum(
            "gnqk,kgd->gnqd", weights, value_head_rows.astype(jnp.float32)
        )
        return (new_max, row_sum, weighted)

    def forward_step(running, inputs):
        packed_block, docs_block, group_index = inputs
        allowed = group_mask(group_index, docs_block)
        running = forward_work(running, packed_block, allowed)
        return (running, None)

    statistics_shape = (KEY_VALUE_HEADS, GROUP_SIZE, sharded_rows)
    start_stats = (
        jnp.full(statistics_shape, -jnp.inf, jnp.float32),
        jnp.zeros(statistics_shape, jnp.float32),
        jnp.zeros(statistics_shape + (HEAD_SIZE,), jnp.float32),
    )
    (row_max, row_sum, weighted), _ = lax.scan(
        forward_step, start_stats, (window_pack, window_docs, group_ids)
    )
    log_total = row_max + jnp.log(row_sum)
    attended = jnp.transpose(weighted / row_sum[..., None], (2, 0, 1, 3)).astype(jnp.bfloat16)
    row_dot = jnp.einsum(
        "qgnd,qgnd->gnq", gradient_heads, attended, preferred_element_type=jnp.float32
    )

    def backward_work(grad_query, packed_block, allowed):
        scores, key_head_rows, value_head_rows = group_scores(packed_block, allowed)
        attend = jnp.exp(scores - log_total[..., None])
        grad_prob = jnp.einsum(
            "qgnd,kgd->gnqk", gradient_heads, value_head_rows, preferred_element_type=jnp.float32
        )
        grad_score = (attend * (grad_prob - row_dot[..., None])).astype(jnp.bfloat16)
        grad_query = grad_query + jnp.einsum(
            "gnqk,kgd->qgnd", grad_score, key_head_rows, preferred_element_type=jnp.float32
        )
        key_gradient = (
            jnp.einsum(
                "gnqk,qgnd->kgd", grad_score, query_head_rows, preferred_element_type=jnp.float32
            )
            * score_scale
        )
        value_gradient = jnp.einsum(
            "gnqk,qgnd->kgd",
            attend.astype(jnp.bfloat16),
            gradient_heads,
            preferred_element_type=jnp.float32,
        )
        partial_value = jnp.concatenate(
            [
                key_gradient.reshape(grouped_rows, KEY_VALUE_HEADS * HEAD_SIZE),
                value_gradient.reshape(grouped_rows, KEY_VALUE_HEADS * HEAD_SIZE),
            ],
            axis=1,
        )
        return (grad_query, partial_value)

    def backward_step(grad_query, inputs):
        packed_block, docs_block, group_index = inputs
        allowed = group_mask(group_index, docs_block)
        return backward_work(grad_query, packed_block, allowed)

    grad_query, partials = lax.scan(
        backward_step,
        jnp.zeros((sharded_rows, KEY_VALUE_HEADS, GROUP_SIZE, HEAD_SIZE), jnp.float32),
        (window_pack, window_docs, group_ids),
    )
    partials = partials.reshape(padded_slots, sharded_rows, packed_width)
    query_grad = (grad_query * score_scale).reshape(sharded_rows, QUERY_HEADS * HEAD_SIZE)

    def return_partial(step_index, running):
        returned = passed_along(running, "ctx", -1)
        return returned + lax.dynamic_index_in_dim(
            partials, window_slots - 1 - step_index, 0, keepdims=False
        )

    summed_total = lax.fori_loop(1, window_slots, return_partial, partials[window_slots - 1])
    key_gradient = summed_total[:, : KEY_VALUE_HEADS * HEAD_SIZE].astype(jnp.bfloat16)
    value_gradient = summed_total[:, KEY_VALUE_HEADS * HEAD_SIZE :].astype(jnp.bfloat16)
    grad_bias = lax.psum(jnp.sum(query_grad, axis=0), ("dp", "ctx"))
    attended_out = attended.reshape(sharded_rows, QUERY_HEADS * HEAD_SIZE)
    return (
        attended_out[None],
        query_grad.astype(jnp.bfloat16)[None],
        key_gradient[None],
        value_gradient[None],
        grad_bias,
    )


def solution(mesh):
    placed = (
        P("dp", "ctx", None),
        P("dp", "ctx", None),
        P("dp", "ctx", None),
        P("dp", "ctx", None),
        P("dp", "ctx"),
        P(),
    )
    return jax.shard_map(
        local,
        mesh=mesh,
        in_specs=placed,
        out_specs=(
            P("dp", "ctx", None),
            P("dp", "ctx", None),
            P("dp", "ctx", None),
            P("dp", "ctx", None),
            P(),
        ),
        check_vma=False,
    )
```

profile of v0, /device:TPU:1, one launch (start us, length us, event | category | flops | bytes accessed | tf_op | source)
XLA Modules:
  0.0 563.7 jit_solution(16847469983181574787)
XLA Ops:
  3.6 2.0 copy.54
  7.4 1.6 concatenate.17
  8.9 138.4 %while.72 = (s32[]{:T(128)}, bf16[16,128,512]{2,1,0:T(8,128)(2,1)}, s32[16,128]{1,0:T(8,128)S(1)}, bf16[128,512]{1,0:T(8,128)(2,1)S(1)}, s32[128]{0:T(128)S(1)}, /*index=5*/s32[]{:T(128)}, s32[]{:T(128)}, s32[]{:T(128)}) while((s32[]{:T(128)}, bf16[16,128,512]{2,1,0:T(8,128)(2,1)}, s32[16,128]{1,0:T(8,128)S(1)}, ...), condition=%wide.region_1.2_spmd, body=%wide.region_0.1_spmd.sunk | while | flops 5 | bytes 1052879 | solution.py:67
  8.9 4.1 collective-permute-start
  13.0 3.1 collective-permute-start.1
  17.5 3.6 collective-permute-start
  21.1 3.1 collective-permute-start.1
  25.7 3.6 collective-permute-start
  29.2 4.8 collective-permute-start.1
  35.5 3.9 collective-permute-start
  39.4 3.7 collective-permute-start.1
  44.5 3.9 collective-permute-start
  48.4 3.7 collective-permute-start.1
  53.5 3.6 collective-permute-start
  57.1 4.0 collective-permute-start.1
  62.6 3.6 collective-permute-start
  66.1 4.0 collective-permute-start.1
  71.6 3.6 collective-permute-start
  75.2 4.0 collective-permute-start.1
  80.6 3.6 collective-permute-start
  84.2 4.0 collective-permute-start.1
  89.7 3.6 collective-permute-start
  93.2 4.3 collective-permute-start.1
  99.0 3.6 collective-permute-start
  102.5 4.8 collective-permute-start.1
  108.8 3.6 collective-permute-start
  112.4 4.3 collective-permute-start.1
  118.1 3.9 collective-permute-start
  122.0 3.7 collective-permute-start.1
  127.1 3.9 collective-permute-start
  131.0 4.5 collective-permute-start.1
  137.0 3.6 collective-permute-start
  140.5 5.3 collective-permute-start.1
  147.3 4.1 copy.51
  151.5 23.1 %while.74 = (s32[]{:T(128)}, f32[2,7,128]{2,1,0:T(8,128)S(1)}, f32[2,7,128]{2,1,0:T(8,128)S(1)}, f32[2,7,128,128]{3,2,1,0:T(8,128)S(1)}, s32[4]{0:T(128)S(1)}, /...) while((s32[]{:T(128)}, f32[2,7,128]{2,1,0:T(8,128)S(1)}, ...), condition=%wide.region_5.6_spmd.clone.clone.clone, body=%wide.region_2.5_spmd.clone.clone.clone.sunk | while | flops 480120704 | bytes 16320205 | solution.py:125
  155.8 1.4 fusion.117
  161.6 1.4 fusion.117
  175.6 1.5 copy.53
  179.3 42.8 %while.75 = (s32[]{:T(128)}, f32[128,2,7,128]{0,3,2,1:T(8,128)S(1)}, f32[4,512,512]{2,1,0:T(8,128)}, bf16[4,512,512]{1,2,0:T(8,128)(2,1)}, s32[4]{0:T(128)S(1)},...) while((s32[]{:T(128)}, ...), condition=%wide.region_7.8_spmd.clone.clone.clone, body=%wide.region_6.7_spmd.clone.clone.clone.sunk | while | flops 1184918656 | bytes 30644960 | solution.py:170
  182.8 2.1 fusion.134
  184.8 2.3 fusion.132
  193.4 2.1 fusion.134
  195.5 2.3 fusion.132
  204.2 2.1 fusion.134
  206.3 2.3 fusion.132
  214.9 2.1 fusion.134
  217.0 2.3 fusion.132
  223.1 163.2 %while.73 = (s32[]{:T(128)}, f32[128,512]{1,0:T(8,128)S(1)}, f32[16,128,512]{2,1,0:T(8,128)}, s32[]{:T(128)}, s32[]{:T(128)}, /*index=5*/s32[]{:T(128)}, s32[]{:T(128)}) while((s32[]{:T(128)}, f32[128,512]{1,0:T(8,128)S(1)}, f32[16,128,512]{2,1,0:T(8,128)}, s32[]{:T(128)}, s32[]{:T(128)}, /*index=5*/s32[]{:T(128)}, s32[]{:T(128)}) %tuple.177), condition=%wide.region_9.10_spmd, body=%wide.region_8.9_spmd.sunk | while | flops 65542 | bytes 1835175 | solution.py:184
  224.4 6.0 %collective-permute-done.2 = f32[128,512]{1,0:T(8,128)S(1)} collective-permute-done((f32[128,512]{1,0:T(8,128)S(1)}, f32[128,512]{1,0:T(8,128)S(1)}, u32[]{:S(2)}, u32[]{:S(2)}) %collective-permute-start.2) | collective-permute-done | bytes 262176 | tf_op jit(solution)/shard_map/while/body/eval_jaxpr/ppermute | solution.py:18
  232.7 7.8 %collective-permute-done.2 = f32[128,512]{1,0:T(8,128)S(1)} collective-permute-done((f32[128,512]{1,0:T(8,128)S(1)}, f32[128,512]{1,0:T(8,128)S(1)}, u32[]{:S(2)}, u32[]{:S(2)}) %collective-permute-start.2) | collective-permute-done | bytes 262176 | tf_op jit(solution)/shard_map/while/body/eval_jaxpr/ppermute | solution.py:18
  242.8 7.7 %collective-permute-done.2 = f32[128,512]{1,0:T(8,128)S(1)} collective-permute-done((f32[128,512]{1,0:T(8,128)S(1)}, f32[128,512]{1,0:T(8,128)S(1)}, u32[]{:S(2)}, u32[]{:S(2)}) %collective-permute-start.2) | collective-permute-done | bytes 262176 | tf_op jit(solution)/shard_map/while/body/eval_jaxpr/ppermute | solution.py:18
  252.8 10.2 %collective-permute-done.2 = f32[128,512]{1,0:T(8,128)S(1)} collective-permute-done((f32[128,512]{1,0:T(8,128)S(1)}, f32[128,512]{1,0:T(8,128)S(1)}, u32[]{:S(2)}, u32[]{:S(2)}) %collective-permute-start.2) | collective-permute-done | bytes 262176 | tf_op jit(solution)/shard_map/while/body/eval_jaxpr/ppermute | solution.py:18
  265.3 11.4 %collective-permute-done.2 = f32[128,512]{1,0:T(8,128)S(1)} collective-permute-done((f32[128,512]{1,0:T(8,128)S(1)}, f32[128,512]{1,0:T(8,128)S(1)}, u32[]{:S(2)}, u32[]{:S(2)}) %collective-permute-start.2) | collective-permute-done | bytes 262176 | tf_op jit(solution)/shard_map/while/body/eval_jaxpr/ppermute | solution.py:18
  279.0 9.2 %collective-permute-done.2 = f32[128,512]{1,0:T(8,128)S(1)} collective-permute-done((f32[128,512]{1,0:T(8,128)S(1)}, f32[128,512]{1,0:T(8,128)S(1)}, u32[]{:S(2)}, u32[]{:S(2)}) %collective-permute-start.2) | collective-permute-done | bytes 262176 | tf_op jit(solution)/shard_map/while/body/eval_jaxpr/ppermute | solution.py:18
  290.5 7.4 %collective-permute-done.2 = f32[128,512]{1,0:T(8,128)S(1)} collective-permute-done((f32[128,512]{1,0:T(8,128)S(1)}, f32[128,512]{1,0:T(8,128)S(1)}, u32[]{:S(2)}, u32[]{:S(2)}) %collective-permute-start.2) | collective-permute-done | bytes 262176 | tf_op jit(solution)/shard_map/while/body/eval_jaxpr/ppermute | solution.py:18
  300.1 6.8 %collective-permute-done.2 = f32[128,512]{1,0:T(8,128)S(1)} collective-permute-done((f32[128,512]{1,0:T(8,128)S(1)}, f32[128,512]{1,0:T(8,128)S(1)}, u32[]{:S(2)}, u32[]{:S(2)}) %collective-permute-start.2) | collective-permute-done | bytes 262176 | tf_op jit(solution)/shard_map/while/body/eval_jaxpr/ppermute | solution.py:18
  309.3 7.6 %collective-permute-done.2 = f32[128,512]{1,0:T(8,128)S(1)} collective-permute-done((f32[128,512]{1,0:T(8,128)S(1)}, f32[128,512]{1,0:T(8,128)S(1)}, u32[]{:S(2)}, u32[]{:S(2)}) %collective-permute-start.2) | collective-permute-done | bytes 262176 | tf_op jit(solution)/shard_map/while/body/eval_jaxpr/ppermute | solution.py:18
  319.2 7.9 %collective-permute-done.2 = f32[128,512]{1,0:T(8,128)S(1)} collective-permute-done((f32[128,512]{1,0:T(8,128)S(1)}, f32[128,512]{1,0:T(8,128)S(1)}, u32[]{:S(2)}, u32[]{:S(2)}) %collective-permute-start.2) | collective-permute-done | bytes 262176 | tf_op jit(solution)/shard_map/while/body/eval_jaxpr/ppermute | solution.py:18
  329.4 7.9 %collective-permute-done.2 = f32[128,512]{1,0:T(8,128)S(1)} collective-permute-done((f32[128,512]{1,0:T(8,128)S(1)}, f32[128,512]{1,0:T(8,128)S(1)}, u32[]{:S(2)}, u32[]{:S(2)}) %collective-permute-start.2) | collective-permute-done | bytes 262176 | tf_op jit(solution)/shard_map/while/body/eval_jaxpr/ppermute | solution.py:18
  339.7 7.9 %collective-permute-done.2 = f32[128,512]{1,0:T(8,128)S(1)} collective-permute-done((f32[128,512]{1,0:T(8,128)S(1)}, f32[128,512]{1,0:T(8,128)S(1)}, u32[]{:S(2)}, u32[]{:S(2)}) %collective-permute-start.2) | collective-permute-done | bytes 262176 | tf_op jit(solution)/shard_map/while/body/eval_jaxpr/ppermute | solution.py:18
  349.9 8.8 %collective-permute-done.2 = f32[128,512]{1,0:T(8,128)S(1)} collective-permute-done((f32[128,512]{1,0:T(8,128)S(1)}, f32[128,512]{1,0:T(8,128)S(1)}, u32[]{:S(2)}, u32[]{:S(2)}) %collective-permute-start.2) | collective-permute-done | bytes 262176 | tf_op jit(solution)/shard_map/while/body/eval_jaxpr/ppermute | solution.py:18
  361.0 10.4 %collective-permute-done.2 = f32[128,512]{1,0:T(8,128)S(1)} collective-permute-done((f32[128,512]{1,0:T(8,128)S(1)}, f32[128,512]{1,0:T(8,128)S(1)}, u32[]{:S(2)}, u32[]{:S(2)}) %collective-permute-start.2) | collective-permute-done | bytes 262176 | tf_op jit(solution)/shard_map/while/body/eval_jaxpr/ppermute | solution.py:18
  373.7 11.5 %collective-permute-done.2 = f32[128,512]{1,0:T(8,128)S(1)} collective-permute-done((f32[128,512]{1,0:T(8,128)S(1)}, f32[128,512]{1,0:T(8,128)S(1)}, u32[]{:S(2)}, u32[]{:S(2)}) %collective-permute-start.2) | collective-permute-done | bytes 262176 | tf_op jit(solution)/shard_map/while/body/eval_jaxpr/ppermute | solution.py:18
  387.3 175.4 %psum.7 = f32[1792]{0:T(1024)} all-reduce(f32[1792]{0:T(1024)S(1)} %reduce_sum.25), channel_id=1, replica_groups=mesh['dp'=8,'ctx'=64] {'dp','ctx'}, use_global_device_ids=true, to_apply=%region_11.12 | all-reduce | flops 1792 | bytes 14336 | tf_op jit(solution)/shard_map/psum | solution.py:187
  (258 shorter events, 105.7 us)
Async XLA Ops:
  8.9 142.6 %copy-start.1 = (s32[1,128]{1,0:T(1,128)S(1)}, s32[1,128]{1,0:T(1,128)}, u32[]{:S(2)}) copy-start(s32[1,128]{1,0:T(1,128)} %param.18) | copy-start | bytes 1540
  8.9 7.9 %collective-permute-start = (bf16[128,512]{1,0:T(8,128)(2,1)S(1)}, bf16[128,512]{1,0:T(8,128)(2,1)S(1)}, u32[]{:S(2)}, u32[]{:S(2)}) collective-permute-start(bf16[128,512]{1,0:T(8,128)(2,1)S(1)} %get-tuple-element.1222), channel_id=1, source_target_pairs={{0,1},{1,2},{2,3},{3,4},{4,5},{5,6},{6,7},{7,8},{8,9},{9,10},{10,1... | collective-permute-start | bytes 393224 | tf_op jit(solution)/shard_map/while/body/eval_jaxpr/ppermute | solution.py:18
  13.0 3.8 collective-permute-start.1
  17.5 7.4 %collective-permute-start = (bf16[128,512]{1,0:T(8,128)(2,1)S(1)}, bf16[128,512]{1,0:T(8,128)(2,1)S(1)}, u32[]{:S(2)}, u32[]{:S(2)}) collective-permute-start(bf16[128,512]{1,0:T(8,128)(2,1)S(1)} %get-tuple-element.1222), channel_id=1, source_target_pairs={{0,1},{1,2},{2,3},{3,4},{4,5},{5,6},{6,7},{7,8},{8,9},{9,10},{10,1... | collective-permute-start | bytes 393224 | tf_op jit(solution)/shard_map/while/body/eval_jaxpr/ppermute | solution.py:18
  21.1 3.8 collective-permute-start.1
  25.7 9.1 %collective-permute-start = (bf16[128,512]{1,0:T(8,128)(2,1)S(1)}, bf16[128,512]{1,0:T(8,128)(2,1)S(1)}, u32[]{:S(2)}, u32[]{:S(2)}) collective-permute-start(bf16[128,512]{1,0:T(8,128)(2,1)S(1)} %get-tuple-element.1222), channel_id=1, source_target_pairs={{0,1},{1,2},{2,3},{3,4},{4,5},{5,6},{6,7},{7,8},{8,9},{9,10},{10,1... | collective-permute-start | bytes 393224 | tf_op jit(solution)/shard_map/while/body/eval_jaxpr/ppermute | solution.py:18
  29.2 5.5 collective-permute-start.1
  35.5 8.3 %collective-permute-start = (bf16[128,512]{1,0:T(8,128)(2,1)S(1)}, bf16[128,512]{1,0:T(8,128)(2,1)S(1)}, u32[]{:S(2)}, u32[]{:S(2)}) collective-permute-start(bf16[128,512]{1,0:T(8,128)(2,1)S(1)} %get-tuple-element.1222), channel_id=1, source_target_pairs={{0,1},{1,2},{2,3},{3,4},{4,5},{5,6},{6,7},{7,8},{8,9},{9,10},{10,1... | collective-permute-start | bytes 393224 | tf_op jit(solution)/shard_map/while/body/eval_jaxpr/ppermute | solution.py:18
  39.4 4.4 collective-permute-start.1
  44.5 8.3 %collective-permute-start = (bf16[128,512]{1,0:T(8,128)(2,1)S(1)}, bf16[128,512]{1,0:T(8,128)(2,1)S(1)}, u32[]{:S(2)}, u32[]{:S(2)}) collective-permute-start(bf16[128,512]{1,0:T(8,128)(2,1)S(1)} %get-tuple-element.1222), channel_id=1, source_target_pairs={{0,1},{1,2},{2,3},{3,4},{4,5},{5,6},{6,7},{7,8},{8,9},{9,10},{10,1... | collective-permute-start | bytes 393224 | tf_op jit(solution)/shard_map/while/body/eval_jaxpr/ppermute | solution.py:18
  48.4 4.4 collective-permute-start.1
  53.5 8.3 %collective-permute-start = (bf16[128,512]{1,0:T(8,128)(2,1)S(1)}, bf16[128,512]{1,0:T(8,128)(2,1)S(1)}, u32[]{:S(2)}, u32[]{:S(2)}) collective-permute-start(bf16[128,512]{1,0:T(8,128)(2,1)S(1)} %get-tuple-element.1222), channel_id=1, source_target_pairs={{0,1},{1,2},{2,3},{3,4},{4,5},{5,6},{6,7},{7,8},{8,9},{9,10},{10,1... | collective-permute-start | bytes 393224 | tf_op jit(solution)/shard_map/while/body/eval_jaxpr/ppermute | solution.py:18
  57.1 4.7 collective-permute-start.1
  62.6 8.3 %collective-permute-start = (bf16[128,512]{1,0:T(8,128)(2,1)S(1)}, bf16[128,512]{1,0:T(8,128)(2,1)S(1)}, u32[]{:S(2)}, u32[]{:S(2)}) collective-permute-start(bf16[128,512]{1,0:T(8,128)(2,1)S(1)} %get-tuple-element.1222), channel_id=1, source_target_pairs={{0,1},{1,2},{2,3},{3,4},{4,5},{5,6},{6,7},{7,8},{8,9},{9,10},{10,1... | collective-permute-start | bytes 393224 | tf_op jit(solution)/shard_map/while/body/eval_jaxpr/ppermute | solution.py:18
  66.1 4.7 collective-permute-start.1
  71.6 8.3 %collective-permute-start = (bf16[128,512]{1,0:T(8,128)(2,1)S(1)}, bf16[128,512]{1,0:T(8,128)(2,1)S(1)}, u32[]{:S(2)}, u32[]{:S(2)}) collective-permute-start(bf16[128,512]{1,0:T(8,128)(2,1)S(1)} %get-tuple-element.1222), channel_id=1, source_target_pairs={{0,1},{1,2},{2,3},{3,4},{4,5},{5,6},{6,7},{7,8},{8,9},{9,10},{10,1... | collective-permute-start | bytes 393224 | tf_op jit(solution)/shard_map/while/body/eval_jaxpr/ppermute | solution.py:18
  75.2 4.7 collective-permute-start.1
  80.6 8.4 %collective-permute-start = (bf16[128,512]{1,0:T(8,128)(2,1)S(1)}, bf16[128,512]{1,0:T(8,128)(2,1)S(1)}, u32[]{:S(2)}, u32[]{:S(2)}) collective-permute-start(bf16[128,512]{1,0:T(8,128)(2,1)S(1)} %get-tuple-element.1222), channel_id=1, source_target_pairs={{0,1},{1,2},{2,3},{3,4},{4,5},{5,6},{6,7},{7,8},{8,9},{9,10},{10,1... | collective-permute-start | bytes 393224 | tf_op jit(solution)/shard_map/while/body/eval_jaxpr/ppermute | solution.py:18
  84.2 4.7 collective-permute-start.1
  89.7 8.6 %collective-permute-start = (bf16[128,512]{1,0:T(8,128)(2,1)S(1)}, bf16[128,512]{1,0:T(8,128)(2,1)S(1)}, u32[]{:S(2)}, u32[]{:S(2)}) collective-permute-start(bf16[128,512]{1,0:T(8,128)(2,1)S(1)} %get-tuple-element.1222), channel_id=1, source_target_pairs={{0,1},{1,2},{2,3},{3,4},{4,5},{5,6},{6,7},{7,8},{8,9},{9,10},{10,1... | collective-permute-start | bytes 393224 | tf_op jit(solution)/shard_map/while/body/eval_jaxpr/ppermute | solution.py:18
  93.2 5.0 collective-permute-start.1
  99.0 9.1 %collective-permute-start = (bf16[128,512]{1,0:T(8,128)(2,1)S(1)}, bf16[128,512]{1,0:T(8,128)(2,1)S(1)}, u32[]{:S(2)}, u32[]{:S(2)}) collective-permute-start(bf16[128,512]{1,0:T(8,128)(2,1)S(1)} %get-tuple-element.1222), channel_id=1, source_target_pairs={{0,1},{1,2},{2,3},{3,4},{4,5},{5,6},{6,7},{7,8},{8,9},{9,10},{10,1... | collective-permute-start | bytes 393224 | tf_op jit(solution)/shard_map/while/body/eval_jaxpr/ppermute | solution.py:18
  102.5 5.5 collective-permute-start.1
  108.8 8.6 %collective-permute-start = (bf16[128,512]{1,0:T(8,128)(2,1)S(1)}, bf16[128,512]{1,0:T(8,128)(2,1)S(1)}, u32[]{:S(2)}, u32[]{:S(2)}) collective-permute-start(bf16[128,512]{1,0:T(8,128)(2,1)S(1)} %get-tuple-element.1222), channel_id=1, source_target_pairs={{0,1},{1,2},{2,3},{3,4},{4,5},{5,6},{6,7},{7,8},{8,9},{9,10},{10,1... | collective-permute-start | bytes 393224 | tf_op jit(solution)/shard_map/while/body/eval_jaxpr/ppermute | solution.py:18
  112.4 5.0 collective-permute-start.1
  118.1 8.3 %collective-permute-start = (bf16[128,512]{1,0:T(8,128)(2,1)S(1)}, bf16[128,512]{1,0:T(8,128)(2,1)S(1)}, u32[]{:S(2)}, u32[]{:S(2)}) collective-permute-start(bf16[128,512]{1,0:T(8,128)(2,1)S(1)} %get-tuple-element.1222), channel_id=1, source_target_pairs={{0,1},{1,2},{2,3},{3,4},{4,5},{5,6},{6,7},{7,8},{8,9},{9,10},{10,1... | collective-permute-start | bytes 393224 | tf_op jit(solution)/shard_map/while/body/eval_jaxpr/ppermute | solution.py:18
  122.0 4.4 collective-permute-start.1
  127.1 9.1 %collective-permute-start = (bf16[128,512]{1,0:T(8,128)(2,1)S(1)}, bf16[128,512]{1,0:T(8,128)(2,1)S(1)}, u32[]{:S(2)}, u32[]{:S(2)}) collective-permute-start(bf16[128,512]{1,0:T(8,128)(2,1)S(1)} %get-tuple-element.1222), channel_id=1, source_target_pairs={{0,1},{1,2},{2,3},{3,4},{4,5},{5,6},{6,7},{7,8},{8,9},{9,10},{10,1... | collective-permute-start | bytes 393224 | tf_op jit(solution)/shard_map/while/body/eval_jaxpr/ppermute | solution.py:18
  131.0 5.2 collective-permute-start.1
  137.0 9.7 %collective-permute-start = (bf16[128,512]{1,0:T(8,128)(2,1)S(1)}, bf16[128,512]{1,0:T(8,128)(2,1)S(1)}, u32[]{:S(2)}, u32[]{:S(2)}) collective-permute-start(bf16[128,512]{1,0:T(8,128)(2,1)S(1)} %get-tuple-element.1222), channel_id=1, source_target_pairs={{0,1},{1,2},{2,3},{3,4},{4,5},{5,6},{6,7},{7,8},{8,9},{9,10},{10,1... | collective-permute-start | bytes 393224 | tf_op jit(solution)/shard_map/while/body/eval_jaxpr/ppermute | solution.py:18
  140.5 6.1 %collective-permute-start.1 = (s32[128]{0:T(128)S(1)}, s32[128]{0:T(128)S(1)}, u32[]{:S(2)}, u32[]{:S(2)}) collective-permute-start(s32[128]{0:T(128)S(1)} %get-tuple-element.1223), channel_id=1, source_target_pairs={{0,1},{1,2},{2,3},{3,4},{4,5},{5,6},{6,7},{7,8},{8,9},{9,10},{10,1... | collective-permute-start | bytes 1544 | tf_op jit(solution)/shard_map/while/body/eval_jaxpr/ppermute | solution.py:18
  174.6 1.0 copy-start
  223.1 7.3 %collective-permute-start.2 = (f32[128,512]{1,0:T(8,128)S(1)}, f32[128,512]{1,0:T(8,128)S(1)}, u32[]{:S(2)}, u32[]{:S(2)}) collective-permute-start(f32[128,512]{1,0:T(8,128)S(1)} %get-tuple-element.1333), channel_id=1, source_target_pairs={{1,0},{2,1},{3,2},{4,3},{5,4},{6,5},{7,6},{8,7},{9,8},{10,9},{11,1... | collective-permute-start | bytes 786440 | tf_op jit(solution)/shard_map/while/body/eval_jaxpr/ppermute | solution.py:18
  231.4 9.1 %collective-permute-start.2 = (f32[128,512]{1,0:T(8,128)S(1)}, f32[128,512]{1,0:T(8,128)S(1)}, u32[]{:S(2)}, u32[]{:S(2)}) collective-permute-start(f32[128,512]{1,0:T(8,128)S(1)} %get-tuple-element.1333), channel_id=1, source_target_pairs={{1,0},{2,1},{3,2},{4,3},{5,4},{6,5},{7,6},{8,7},{9,8},{10,9},{11,1... | collective-permute-start | bytes 786440 | tf_op jit(solution)/shard_map/while/body/eval_jaxpr/ppermute | solution.py:18
  241.5 9.0 %collective-permute-start.2 = (f32[128,512]{1,0:T(8,128)S(1)}, f32[128,512]{1,0:T(8,128)S(1)}, u32[]{:S(2)}, u32[]{:S(2)}) collective-permute-start(f32[128,512]{1,0:T(8,128)S(1)} %get-tuple-element.1333), channel_id=1, source_target_pairs={{1,0},{2,1},{3,2},{4,3},{5,4},{6,5},{7,6},{8,7},{9,8},{10,9},{11,1... | collective-permute-start | bytes 786440 | tf_op jit(solution)/shard_map/while/body/eval_jaxpr/ppermute | solution.py:18
  251.5 11.5 %collective-permute-start.2 = (f32[128,512]{1,0:T(8,128)S(1)}, f32[128,512]{1,0:T(8,128)S(1)}, u32[]{:S(2)}, u32[]{:S(2)}) collective-permute-start(f32[128,512]{1,0:T(8,128)S(1)} %get-tuple-element.1333), channel_id=1, source_target_pairs={{1,0},{2,1},{3,2},{4,3},{5,4},{6,5},{7,6},{8,7},{9,8},{10,9},{11,1... | collective-permute-start | bytes 786440 | tf_op jit(solution)/shard_map/while/body/eval_jaxpr/ppermute | solution.py:18
  264.0 12.7 %collective-permute-start.2 = (f32[128,512]{1,0:T(8,128)S(1)}, f32[128,512]{1,0:T(8,128)S(1)}, u32[]{:S(2)}, u32[]{:S(2)}) collective-permute-start(f32[128,512]{1,0:T(8,128)S(1)} %get-tuple-element.1333), channel_id=1, source_target_pairs={{1,0},{2,1},{3,2},{4,3},{5,4},{6,5},{7,6},{8,7},{9,8},{10,9},{11,1... | collective-permute-start | bytes 786440 | tf_op jit(solution)/shard_map/while/body/eval_jaxpr/ppermute | solution.py:18
  277.7 10.5 %collective-permute-start.2 = (f32[128,512]{1,0:T(8,128)S(1)}, f32[128,512]{1,0:T(8,128)S(1)}, u32[]{:S(2)}, u32[]{:S(2)}) collective-permute-start(f32[128,512]{1,0:T(8,128)S(1)} %get-tuple-element.1333), channel_id=1, source_target_pairs={{1,0},{2,1},{3,2},{4,3},{5,4},{6,5},{7,6},{8,7},{9,8},{10,9},{11,1... | collective-permute-start | bytes 786440 | tf_op jit(solution)/shard_map/while/body/eval_jaxpr/ppermute | solution.py:18
  289.2 8.7 %collective-permute-start.2 = (f32[128,512]{1,0:T(8,128)S(1)}, f32[128,512]{1,0:T(8,128)S(1)}, u32[]{:S(2)}, u32[]{:S(2)}) collective-permute-start(f32[128,512]{1,0:T(8,128)S(1)} %get-tuple-element.1333), channel_id=1, source_target_pairs={{1,0},{2,1},{3,2},{4,3},{5,4},{6,5},{7,6},{8,7},{9,8},{10,9},{11,1... | collective-permute-start | bytes 786440 | tf_op jit(solution)/shard_map/while/body/eval_jaxpr/ppermute | solution.py:18
  298.8 8.1 %collective-permute-start.2 = (f32[128,512]{1,0:T(8,128)S(1)}, f32[128,512]{1,0:T(8,128)S(1)}, u32[]{:S(2)}, u32[]{:S(2)}) collective-permute-start(f32[128,512]{1,0:T(8,128)S(1)} %get-tuple-element.1333), channel_id=1, source_target_pairs={{1,0},{2,1},{3,2},{4,3},{5,4},{6,5},{7,6},{8,7},{9,8},{10,9},{11,1... | collective-permute-start | bytes 786440 | tf_op jit(solution)/shard_map/while/body/eval_jaxpr/ppermute | solution.py:18
  308.0 8.9 %collective-permute-start.2 = (f32[128,512]{1,0:T(8,128)S(1)}, f32[128,512]{1,0:T(8,128)S(1)}, u32[]{:S(2)}, u32[]{:S(2)}) collective-permute-start(f32[128,512]{1,0:T(8,128)S(1)} %get-tuple-element.1333), channel_id=1, source_target_pairs={{1,0},{2,1},{3,2},{4,3},{5,4},{6,5},{7,6},{8,7},{9,8},{10,9},{11,1... | collective-permute-start | bytes 786440 | tf_op jit(solution)/shard_map/while/body/eval_jaxpr/ppermute | solution.py:18
  317.9 9.2 %collective-permute-start.2 = (f32[128,512]{1,0:T(8,128)S(1)}, f32[128,512]{1,0:T(8,128)S(1)}, u32[]{:S(2)}, u32[]{:S(2)}) collective-permute-start(f32[128,512]{1,0:T(8,128)S(1)} %get-tuple-element.1333), channel_id=1, source_target_pairs={{1,0},{2,1},{3,2},{4,3},{5,4},{6,5},{7,6},{8,7},{9,8},{10,9},{11,1... | collective-permute-start | bytes 786440 | tf_op jit(solution)/shard_map/while/body/eval_jaxpr/ppermute | solution.py:18
  328.1 9.2 %collective-permute-start.2 = (f32[128,512]{1,0:T(8,128)S(1)}, f32[128,512]{1,0:T(8,128)S(1)}, u32[]{:S(2)}, u32[]{:S(2)}) collective-permute-start(f32[128,512]{1,0:T(8,128)S(1)} %get-tuple-element.1333), channel_id=1, source_target_pairs={{1,0},{2,1},{3,2},{4,3},{5,4},{6,5},{7,6},{8,7},{9,8},{10,9},{11,1... | collective-permute-start | bytes 786440 | tf_op jit(solution)/shard_map/while/body/eval_jaxpr/ppermute | solution.py:18
  338.4 9.2 %collective-permute-start.2 = (f32[128,512]{1,0:T(8,128)S(1)}, f32[128,512]{1,0:T(8,128)S(1)}, u32[]{:S(2)}, u32[]{:S(2)}) collective-permute-start(f32[128,512]{1,0:T(8,128)S(1)} %get-tuple-element.1333), channel_id=1, source_target_pairs={{1,0},{2,1},{3,2},{4,3},{5,4},{6,5},{7,6},{8,7},{9,8},{10,9},{11,1... | collective-permute-start | bytes 786440 | tf_op jit(solution)/shard_map/while/body/eval_jaxpr/ppermute | solution.py:18
  348.6 10.1 %collective-permute-start.2 = (f32[128,512]{1,0:T(8,128)S(1)}, f32[128,512]{1,0:T(8,128)S(1)}, u32[]{:S(2)}, u32[]{:S(2)}) collective-permute-start(f32[128,512]{1,0:T(8,128)S(1)} %get-tuple-element.1333), channel_id=1, source_target_pairs={{1,0},{2,1},{3,2},{4,3},{5,4},{6,5},{7,6},{8,7},{9,8},{10,9},{11,1... | collective-permute-start | bytes 786440 | tf_op jit(solution)/shard_map/while/body/eval_jaxpr/ppermute | solution.py:18
  359.7 11.7 %collective-permute-start.2 = (f32[128,512]{1,0:T(8,128)S(1)}, f32[128,512]{1,0:T(8,128)S(1)}, u32[]{:S(2)}, u32[]{:S(2)}) collective-permute-start(f32[128,512]{1,0:T(8,128)S(1)} %get-tuple-element.1333), channel_id=1, source_target_pairs={{1,0},{2,1},{3,2},{4,3},{5,4},{6,5},{7,6},{8,7},{9,8},{10,9},{11,1... | collective-permute-start | bytes 786440 | tf_op jit(solution)/shard_map/while/body/eval_jaxpr/ppermute | solution.py:18
  372.4 12.8 %collective-permute-start.2 = (f32[128,512]{1,0:T(8,128)S(1)}, f32[128,512]{1,0:T(8,128)S(1)}, u32[]{:S(2)}, u32[]{:S(2)}) collective-permute-start(f32[128,512]{1,0:T(8,128)S(1)} %get-tuple-element.1333), channel_id=1, source_target_pairs={{1,0},{2,1},{3,2},{4,3},{5,4},{6,5},{7,6},{8,7},{9,8},{10,9},{11,1... | collective-permute-start | bytes 786440 | tf_op jit(solution)/shard_map/while/body/eval_jaxpr/ppermute | solution.py:18
where the time goes:
time: 567 us; the launch traced here: 564 us
  blocking collectives  175 us (31%)
  waiting for transfers between devices  139 us (25%)
  starting transfers between devices  136 us (24%)
  local copies, waits for them, and re-layouts  47.1 us (8%)
  matrix products  34.2 us (6%)
  other arithmetic  24 us (4%)
  loops' own time  6.87 us (1%)
    psum x1, blocking collectives, local(): grad_bias = lax.psum(jnp.sum(query_grad, axis=0), ('dp', 'ctx'))  175 us
    ppermute x45, waiting for transfers between devices, passed_along(): lax.ppermute(value, axis, [(source, source + steps) for source in range(f...  139 us
    ppermute x45, starting transfers between devices, passed_along(): lax.ppermute(value, axis, [(source, source + steps) for source in range(f...  136 us
    add x15, other arithmetic, return_partial(): returned + lax.dynamic_index_in_dim(partials, window_slots - 1 - step_ind...  14.8 us
  transfers between devices with their start and end apart: 45, of which 30 were waited for; matrix products, arithmetic and copies ran while one was open for 0% of the time, Pallas kernels for 0%

commit v1 on v0

--- a/solution.py
+++ b/solution.py
@@ -184,7 +184,10 @@
     summed_total = lax.fori_loop(1, window_slots, return_partial, partials[window_slots - 1])
     key_gradient = summed_total[:, : KEY_VALUE_HEADS * HEAD_SIZE].astype(jnp.bfloat16)
     value_gradient = summed_total[:, KEY_VALUE_HEADS * HEAD_SIZE :].astype(jnp.bfloat16)
-    grad_bias = lax.psum(jnp.sum(query_grad, axis=0), ("dp", "ctx"))
+    choose_the_columns = lambda base_x, axis_key, net_axis: lax.psum(
+        lax.psum(base_x, axis_key), net_axis
+    )
+    grad_bias = choose_the_columns(jnp.sum(query_grad, axis=0), "dp", "ctx")
     attended_out = attended.reshape(sharded_rows, QUERY_HEADS * HEAD_SIZE)
     return (
         attended_out[None],

time: 567 us -> 615 us (1.085)
  the two profiles are of different devices: /device:TPU:1 before, /device:TPU:256 now
where the time goes in v1:
time: 615 us; the launch traced here: 612 us
  starting transfers between devices  170 us (28%)
  waiting for transfers between devices  170 us (28%)
  blocking collectives  159 us (26%)
  local copies, waits for them, and re-layouts  47 us (8%)
  matrix products  34.2 us (6%)
  other arithmetic  23.9 us (4%)
  loops' own time  6.9 us (1%)
    ppermute x45, waiting for transfers between devices, passed_along(): lax.ppermute(value, axis, [(source, source + steps) for source in range(f...  170 us
    ppermute x45, starting transfers between devices, passed_along(): lax.ppermute(value, axis, [(source, source + steps) for source in range(f...  170 us
    psum x1, blocking collectives, local(): lax.psum(lax.psum(base_x, axis_key), net_axis)  146 us
    add x15, other arithmetic, return_partial(): returned + lax.dynamic_index_in_dim(partials, window_slots - 1 - step_ind...  14.8 us
    psum x1, blocking collectives, local(): lax.psum(base_x, axis_key)  12.7 us
  transfers between devices with their start and end apart: 45, of which 30 were waited for; matrix products, arithmetic and copies ran while one was open for 0% of the time, Pallas kernels for 0%

profile of v1, /device:TPU:256, one launch (start us, length us, event | category | flops | bytes accessed | tf_op | source)
XLA Modules:
  0.0 612.0 jit_solution(8247892324866899004)
XLA Ops:
  3.6 2.0 copy.54
  8.9 173.2 %while.72 = (s32[]{:T(128)}, bf16[16,128,512]{2,1,0:T(8,128)(2,1)}, s32[16,128]{1,0:T(8,128)S(1)}, bf16[128,512]{1,0:T(8,128)(2,1)S(1)}, s32[128]{0:T(128)S(1)}, /*index=5*/s32[]{:T(128)}, s32[]{:T(128)}, s32[]{:T(128)}) while((s32[]{:T(128)}, bf16[16,128,512]{2,1,0:T(8,128)(2,1)}, s32[16,128]{1,0:T(8,128)S(1)}, ...), condition=%wide.region_1.2_spmd, body=%wide.region_0.1_spmd.sunk | while | flops 5 | bytes 1052879 | solution.py:67
  8.9 3.5 collective-permute-start
  12.4 3.4 collective-permute-start.1
  15.8 5.3 collective-permute-done.1
  25.7 6.8 %collective-permute-done.1 = s32[128]{0:T(128)S(1)} collective-permute-done((s32[128]{0:T(128)S(1)}, s32[128]{0:T(128)S(1)}, u32[]{:S(2)}, u32[]{:S(2)}) %collective-permute-start.1) | collective-permute-done | bytes 544 | tf_op jit(solution)/shard_map/while/body/eval_jaxpr/ppermute | solution.py:18
  37.1 6.8 %collective-permute-done.1 = s32[128]{0:T(128)S(1)} collective-permute-done((s32[128]{0:T(128)S(1)}, s32[128]{0:T(128)S(1)}, u32[]{:S(2)}, u32[]{:S(2)}) %collective-permute-start.1) | collective-permute-done | bytes 544 | tf_op jit(solution)/shard_map/while/body/eval_jaxpr/ppermute | solution.py:18
  48.5 6.8 %collective-permute-done.1 = s32[128]{0:T(128)S(1)} collective-permute-done((s32[128]{0:T(128)S(1)}, s32[128]{0:T(128)S(1)}, u32[]{:S(2)}, u32[]{:S(2)}) %collective-permute-start.1) | collective-permute-done | bytes 544 | tf_op jit(solution)/shard_map/while/body/eval_jaxpr/ppermute | solution.py:18
  59.9 6.8 %collective-permute-done.1 = s32[128]{0:T(128)S(1)} collective-permute-done((s32[128]{0:T(128)S(1)}, s32[128]{0:T(128)S(1)}, u32[]{:S(2)}, u32[]{:S(2)}) %collective-permute-start.1) | collective-permute-done | bytes 544 | tf_op jit(solution)/shard_map/while/body/eval_jaxpr/ppermute | solution.py:18
  71.3 6.8 %collective-permute-done.1 = s32[128]{0:T(128)S(1)} collective-permute-done((s32[128]{0:T(128)S(1)}, s32[128]{0:T(128)S(1)}, u32[]{:S(2)}, u32[]{:S(2)}) %collective-permute-start.1) | collective-permute-done | bytes 544 | tf_op jit(solution)/shard_map/while/body/eval_jaxpr/ppermute | solution.py:18
  82.7 6.8 %collective-permute-done.1 = s32[128]{0:T(128)S(1)} collective-permute-done((s32[128]{0:T(128)S(1)}, s32[128]{0:T(128)S(1)}, u32[]{:S(2)}, u32[]{:S(2)}) %collective-permute-start.1) | collective-permute-done | bytes 544 | tf_op jit(solution)/shard_map/while/body/eval_jaxpr/ppermute | solution.py:18
  92.1 1.9 collective-permute-start.1
  94.1 7.0 %collective-permute-done.1 = s32[128]{0:T(128)S(1)} collective-permute-done((s32[128]{0:T(128)S(1)}, s32[128]{0:T(128)S(1)}, u32[]{:S(2)}, u32[]{:S(2)}) %collective-permute-start.1) | collective-permute-done | bytes 544 | tf_op jit(solution)/shard_map/while/body/eval_jaxpr/ppermute | solution.py:18
  105.7 7.4 %collective-permute-done.1 = s32[128]{0:T(128)S(1)} collective-permute-done((s32[128]{0:T(128)S(1)}, s32[128]{0:T(128)S(1)}, u32[]{:S(2)}, u32[]{:S(2)}) %collective-permute-start.1) | collective-permute-done | bytes 544 | tf_op jit(solution)/shard_map/while/body/eval_jaxpr/ppermute | solution.py:18
  117.6 6.8 %collective-permute-done.1 = s32[128]{0:T(128)S(1)} collective-permute-done((s32[128]{0:T(128)S(1)}, s32[128]{0:T(128)S(1)}, u32[]{:S(2)}, u32[]{:S(2)}) %collective-permute-start.1) | collective-permute-done | bytes 544 | tf_op jit(solution)/shard_map/while/body/eval_jaxpr/ppermute | solution.py:18
  129.0 6.8 %collective-permute-done.1 = s32[128]{0:T(128)S(1)} collective-permute-done((s32[128]{0:T(128)S(1)}, s32[128]{0:T(128)S(1)}, u32[]{:S(2)}, u32[]{:S(2)}) %collective-permute-start.1) | collective-permute-done | bytes 544 | tf_op jit(solution)/shard_map/while/body/eval_jaxpr/ppermute | solution.py:18
  140.4 6.8 %collective-permute-done.1 = s32[128]{0:T(128)S(1)} collective-permute-done((s32[128]{0:T(128)S(1)}, s32[128]{0:T(128)S(1)}, u32[]{:S(2)}, u32[]{:S(2)}) %collective-permute-start.1) | collective-permute-done | bytes 544 | tf_op jit(solution)/shard_map/while/body/eval_jaxpr/ppermute | solution.py:18
  151.8 6.8 %collective-permute-done.1 = s32[128]{0:T(128)S(1)} collective-permute-done((s32[128]{0:T(128)S(1)}, s32[128]{0:T(128)S(1)}, u32[]{:S(2)}, u32[]{:S(2)}) %collective-permute-start.1) | collective-permute-done | bytes 544 | tf_op jit(solution)/shard_map/while/body/eval_jaxpr/ppermute | solution.py:18
  163.2 6.8 %collective-permute-done.1 = s32[128]{0:T(128)S(1)} collective-permute-done((s32[128]{0:T(128)S(1)}, s32[128]{0:T(128)S(1)}, u32[]{:S(2)}, u32[]{:S(2)}) %collective-permute-start.1) | collective-permute-done | bytes 544 | tf_op jit(solution)/shard_map/while/body/eval_jaxpr/ppermute | solution.py:18
  174.6 6.8 %collective-permute-done.1 = s32[128]{0:T(128)S(1)} collective-permute-done((s32[128]{0:T(128)S(1)}, s32[128]{0:T(128)S(1)}, u32[]{:S(2)}, u32[]{:S(2)}) %collective-permute-start.1) | collective-permute-done | bytes 544 | tf_op jit(solution)/shard_map/while/body/eval_jaxpr/ppermute | solution.py:18
  182.1 4.1 copy.51
  186.2 23.1 %while.74 = (s32[]{:T(128)}, f32[2,7,128]{2,1,0:T(8,128)S(1)}, f32[2,7,128]{2,1,0:T(8,128)S(1)}, f32[2,7,128,128]{3,2,1,0:T(8,128)S(1)}, s32[4]{0:T(128)S(1)}, /...) while((s32[]{:T(128)}, f32[2,7,128]{2,1,0:T(8,128)S(1)}, ...), condition=%wide.region_5.6_spmd.clone.clone.clone, body=%wide.region_2.5_spmd.clone.clone.clone.sunk | while | flops 480120704 | bytes 16320205 | solution.py:125
  214.0 42.8 %while.75 = (s32[]{:T(128)}, f32[128,2,7,128]{0,3,2,1:T(8,128)S(1)}, f32[4,512,512]{2,1,0:T(8,128)}, bf16[4,512,512]{1,2,0:T(8,128)(2,1)}, s32[4]{0:T(128)S(1)},...) while((s32[]{:T(128)}, ...), condition=%wide.region_7.8_spmd.clone.clone.clone, body=%wide.region_6.7_spmd.clone.clone.clone.sunk | while | flops 1184918656 | bytes 30644960 | solution.py:170
  217.5 2.1 fusion.134
  219.6 2.3 fusion.132
  228.2 2.1 fusion.134
  230.2 2.3 fusion.132
  238.9 2.1 fusion.134
  241.0 2.3 fusion.132
  249.6 2.1 fusion.134
  251.7 2.3 fusion.132
  257.8 193.2 %while.73 = (s32[]{:T(128)}, f32[128,512]{1,0:T(8,128)S(1)}, f32[16,128,512]{2,1,0:T(8,128)}, s32[]{:T(128)}, s32[]{:T(128)}, /*index=5*/s32[]{:T(128)}, s32[]{:T(128)}) while((s32[]{:T(128)}, f32[128,512]{1,0:T(8,128)S(1)}, f32[16,128,512]{2,1,0:T(8,128)}, s32[]{:T(128)}, s32[]{:T(128)}, /*index=5*/s32[]{:T(128)}, s32[]{:T(128)}) %tuple.177), condition=%wide.region_9.10_spmd, body=%wide.region_8.9_spmd.sunk | while | flops 65542 | bytes 1835175 | solution.py:184
  257.8 3.9 collective-permute-start.2
  261.7 6.1 collective-permute-done.2
  268.8 5.5 collective-permute-start.2
  274.3 4.0 collective-permute-done.2
  279.3 7.6 %collective-permute-start.2 = (f32[128,512]{1,0:T(8,128)S(1)}, f32[128,512]{1,0:T(8,128)S(1)}, u32[]{:S(2)}, u32[]{:S(2)}) collective-permute-start(f32[128,512]{1,0:T(8,128)S(1)} %get-tuple-element.1333), channel_id=1, source_target_pairs={{1,0},{2,1},{3,2},{4,3},{5,4},{6,5},{7,6},{8,7},{9,8},{10,9},{11,1... | collective-permute-start | bytes 786440 | tf_op jit(solution)/shard_map/while/body/eval_jaxpr/ppermute | solution.py:18
  286.9 4.4 collective-permute-done.2
  292.2 7.7 %collective-permute-start.2 = (f32[128,512]{1,0:T(8,128)S(1)}, f32[128,512]{1,0:T(8,128)S(1)}, u32[]{:S(2)}, u32[]{:S(2)}) collective-permute-start(f32[128,512]{1,0:T(8,128)S(1)} %get-tuple-element.1333), channel_id=1, source_target_pairs={{1,0},{2,1},{3,2},{4,3},{5,4},{6,5},{7,6},{8,7},{9,8},{10,9},{11,1... | collective-permute-start | bytes 786440 | tf_op jit(solution)/shard_map/while/body/eval_jaxpr/ppermute | solution.py:18
  300.0 5.5 collective-permute-done.2
  306.5 7.7 %collective-permute-start.2 = (f32[128,512]{1,0:T(8,128)S(1)}, f32[128,512]{1,0:T(8,128)S(1)}, u32[]{:S(2)}, u32[]{:S(2)}) collective-permute-start(f32[128,512]{1,0:T(8,128)S(1)} %get-tuple-element.1333), channel_id=1, source_target_pairs={{1,0},{2,1},{3,2},{4,3},{5,4},{6,5},{7,6},{8,7},{9,8},{10,9},{11,1... | collective-permute-start | bytes 786440 | tf_op jit(solution)/shard_map/while/body/eval_jaxpr/ppermute | solution.py:18
  314.2 6.6 %collective-permute-done.2 = f32[128,512]{1,0:T(8,128)S(1)} collective-permute-done((f32[128,512]{1,0:T(8,128)S(1)}, f32[128,512]{1,0:T(8,128)S(1)}, u32[]{:S(2)}, u32[]{:S(2)}) %collective-permute-start.2) | collective-permute-done | bytes 262176 | tf_op jit(solution)/shard_map/while/body/eval_jaxpr/ppermute | solution.py:18
  321.8 7.7 %collective-permute-start.2 = (f32[128,512]{1,0:T(8,128)S(1)}, f32[128,512]{1,0:T(8,128)S(1)}, u32[]{:S(2)}, u32[]{:S(2)}) collective-permute-start(f32[128,512]{1,0:T(8,128)S(1)} %get-tuple-element.1333), channel_id=1, source_target_pairs={{1,0},{2,1},{3,2},{4,3},{5,4},{6,5},{7,6},{8,7},{9,8},{10,9},{11,1... | collective-permute-start | bytes 786440 | tf_op jit(solution)/shard_map/while/body/eval_jaxpr/ppermute | solution.py:18
  329.5 5.8 collective-permute-done.2
  336.3 7.7 %collective-permute-start.2 = (f32[128,512]{1,0:T(8,128)S(1)}, f32[128,512]{1,0:T(8,128)S(1)}, u32[]{:S(2)}, u32[]{:S(2)}) collective-permute-start(f32[128,512]{1,0:T(8,128)S(1)} %get-tuple-element.1333), channel_id=1, source_target_pairs={{1,0},{2,1},{3,2},{4,3},{5,4},{6,5},{7,6},{8,7},{9,8},{10,9},{11,1... | collective-permute-start | bytes 786440 | tf_op jit(solution)/shard_map/while/body/eval_jaxpr/ppermute | solution.py:18
  344.1 5.0 collective-permute-done.2
  350.1 7.7 %collective-permute-start.2 = (f32[128,512]{1,0:T(8,128)S(1)}, f32[128,512]{1,0:T(8,128)S(1)}, u32[]{:S(2)}, u32[]{:S(2)}) collective-permute-start(f32[128,512]{1,0:T(8,128)S(1)} %get-tuple-element.1333), channel_id=1, source_target_pairs={{1,0},{2,1},{3,2},{4,3},{5,4},{6,5},{7,6},{8,7},{9,8},{10,9},{11,1... | collective-permute-start | bytes 786440 | tf_op jit(solution)/shard_map/while/body/eval_jaxpr/ppermute | solution.py:18
  357.8 4.1 collective-permute-done.2
  362.8 7.7 %collective-permute-start.2 = (f32[128,512]{1,0:T(8,128)S(1)}, f32[128,512]{1,0:T(8,128)S(1)}, u32[]{:S(2)}, u32[]{:S(2)}) collective-permute-start(f32[128,512]{1,0:T(8,128)S(1)} %get-tuple-element.1333), channel_id=1, source_target_pairs={{1,0},{2,1},{3,2},{4,3},{5,4},{6,5},{7,6},{8,7},{9,8},{10,9},{11,1... | collective-permute-start | bytes 786440 | tf_op jit(solution)/shard_map/while/body/eval_jaxpr/ppermute | solution.py:18
  370.6 3.9 collective-permute-done.2
  375.4 7.7 %collective-permute-start.2 = (f32[128,512]{1,0:T(8,128)S(1)}, f32[128,512]{1,0:T(8,128)S(1)}, u32[]{:S(2)}, u32[]{:S(2)}) collective-permute-start(f32[128,512]{1,0:T(8,128)S(1)} %get-tuple-element.1333), channel_id=1, source_target_pairs={{1,0},{2,1},{3,2},{4,3},{5,4},{6,5},{7,6},{8,7},{9,8},{10,9},{11,1... | collective-permute-start | bytes 786440 | tf_op jit(solution)/shard_map/while/body/eval_jaxpr/ppermute | solution.py:18
  383.1 3.9 collective-permute-done.2
  388.0 7.7 %collective-permute-start.2 = (f32[128,512]{1,0:T(8,128)S(1)}, f32[128,512]{1,0:T(8,128)S(1)}, u32[]{:S(2)}, u32[]{:S(2)}) collective-permute-start(f32[128,512]{1,0:T(8,128)S(1)} %get-tuple-element.1333), channel_id=1, source_target_pairs={{1,0},{2,1},{3,2},{4,3},{5,4},{6,5},{7,6},{8,7},{9,8},{10,9},{11,1... | collective-permute-start | bytes 786440 | tf_op jit(solution)/shard_map/while/body/eval_jaxpr/ppermute | solution.py:18
  395.7 3.9 collective-permute-done.2
  400.6 7.7 %collective-permute-start.2 = (f32[128,512]{1,0:T(8,128)S(1)}, f32[128,512]{1,0:T(8,128)S(1)}, u32[]{:S(2)}, u32[]{:S(2)}) collective-permute-start(f32[128,512]{1,0:T(8,128)S(1)} %get-tuple-element.1333), channel_id=1, source_target_pairs={{1,0},{2,1},{3,2},{4,3},{5,4},{6,5},{7,6},{8,7},{9,8},{10,9},{11,1... | collective-permute-start | bytes 786440 | tf_op jit(solution)/shard_map/while/body/eval_jaxpr/ppermute | solution.py:18
  408.3 3.9 collective-permute-done.2
  413.2 7.7 %collective-permute-start.2 = (f32[128,512]{1,0:T(8,128)S(1)}, f32[128,512]{1,0:T(8,128)S(1)}, u32[]{:S(2)}, u32[]{:S(2)}) collective-permute-start(f32[128,512]{1,0:T(8,128)S(1)} %get-tuple-element.1333), channel_id=1, source_target_pairs={{1,0},{2,1},{3,2},{4,3},{5,4},{6,5},{7,6},{8,7},{9,8},{10,9},{11,1... | collective-permute-start | bytes 786440 | tf_op jit(solution)/shard_map/while/body/eval_jaxpr/ppermute | solution.py:18
  420.9 3.9 collective-permute-done.2
  425.8 7.7 %collective-permute-start.2 = (f32[128,512]{1,0:T(8,128)S(1)}, f32[128,512]{1,0:T(8,128)S(1)}, u32[]{:S(2)}, u32[]{:S(2)}) collective-permute-start(f32[128,512]{1,0:T(8,128)S(1)} %get-tuple-element.1333), channel_id=1, source_target_pairs={{1,0},{2,1},{3,2},{4,3},{5,4},{6,5},{7,6},{8,7},{9,8},{10,9},{11,1... | collective-permute-start | bytes 786440 | tf_op jit(solution)/shard_map/while/body/eval_jaxpr/ppermute | solution.py:18
  433.5 3.9 collective-permute-done.2
  438.4 7.7 %collective-permute-start.2 = (f32[128,512]{1,0:T(8,128)S(1)}, f32[128,512]{1,0:T(8,128)S(1)}, u32[]{:S(2)}, u32[]{:S(2)}) collective-permute-start(f32[128,512]{1,0:T(8,128)S(1)} %get-tuple-element.1333), channel_id=1, source_target_pairs={{1,0},{2,1},{3,2},{4,3},{5,4},{6,5},{7,6},{8,7},{9,8},{10,9},{11,1... | collective-permute-start | bytes 786440 | tf_op jit(solution)/shard_map/while/body/eval_jaxpr/ppermute | solution.py:18
  446.1 3.9 collective-permute-done.2
  452.0 12.7 %psum.14 = f32[1792]{0:T(1024)S(1)} all-reduce(f32[1792]{0:T(1024)S(1)} %reduce_sum.25), channel_id=1, replica_groups=mesh['dp'=8,'ctx'=64] {'dp'}, use_global_device_ids=true, to_apply=%region_11.12 | all-reduce | flops 1792 | bytes 14336 | tf_op jit(solution)/shard_map/psum | solution.py:188
  464.6 146.4 %psum.15 = f32[1792]{0:T(1024)} all-reduce(f32[1792]{0:T(1024)S(1)} %psum.14), channel_id=1, replica_groups=mesh['dp'=8,'ctx'=64] {'ctx'}, use_global_device_ids=true, to_apply=%region_12.13 | all-reduce | flops 1792 | bytes 14336 | tf_op jit(solution)/shard_map/psum | solution.py:187
  (259 shorter events, 133.2 us)
Async XLA Ops:
  8.9 177.3 %copy-start.1 = (s32[1,128]{1,0:T(1,128)S(1)}, s32[1,128]{1,0:T(1,128)}, u32[]{:S(2)}) copy-start(s32[1,128]{1,0:T(1,128)} %param.18) | copy-start | bytes 1540
  8.9 12.3 %collective-permute-start = (bf16[128,512]{1,0:T(8,128)(2,1)S(1)}, bf16[128,512]{1,0:T(8,128)(2,1)S(1)}, u32[]{:S(2)}, u32[]{:S(2)}) collective-permute-start(bf16[128,512]{1,0:T(8,128)(2,1)S(1)} %get-tuple-element.1222), channel_id=1, source_target_pairs={{0,1},{1,2},{2,3},{3,4},{4,5},{5,6},{6,7},{7,8},{8,9},{9,10},{10,1... | collective-permute-start | bytes 393224 | tf_op jit(solution)/shard_map/while/body/eval_jaxpr/ppermute | solution.py:18
  12.4 8.8 %collective-permute-start.1 = (s32[128]{0:T(128)S(1)}, s32[128]{0:T(128)S(1)}, u32[]{:S(2)}, u32[]{:S(2)}) collective-permute-start(s32[128]{0:T(128)S(1)} %get-tuple-element.1223), channel_id=1, source_target_pairs={{0,1},{1,2},{2,3},{3,4},{4,5},{5,6},{6,7},{7,8},{8,9},{9,10},{10,1... | collective-permute-start | bytes 1544 | tf_op jit(solution)/shard_map/while/body/eval_jaxpr/ppermute | solution.py:18
  21.9 10.7 %collective-permute-start = (bf16[128,512]{1,0:T(8,128)(2,1)S(1)}, bf16[128,512]{1,0:T(8,128)(2,1)S(1)}, u32[]{:S(2)}, u32[]{:S(2)}) collective-permute-start(bf16[128,512]{1,0:T(8,128)(2,1)S(1)} %get-tuple-element.1222), channel_id=1, source_target_pairs={{0,1},{1,2},{2,3},{3,4},{4,5},{5,6},{6,7},{7,8},{8,9},{9,10},{10,1... | collective-permute-start | bytes 393224 | tf_op jit(solution)/shard_map/while/body/eval_jaxpr/ppermute | solution.py:18
  23.8 8.8 %collective-permute-start.1 = (s32[128]{0:T(128)S(1)}, s32[128]{0:T(128)S(1)}, u32[]{:S(2)}, u32[]{:S(2)}) collective-permute-start(s32[128]{0:T(128)S(1)} %get-tuple-element.1223), channel_id=1, source_target_pairs={{0,1},{1,2},{2,3},{3,4},{4,5},{5,6},{6,7},{7,8},{8,9},{9,10},{10,1... | collective-permute-start | bytes 1544 | tf_op jit(solution)/shard_map/while/body/eval_jaxpr/ppermute | solution.py:18
  33.3 10.7 %collective-permute-start = (bf16[128,512]{1,0:T(8,128)(2,1)S(1)}, bf16[128,512]{1,0:T(8,128)(2,1)S(1)}, u32[]{:S(2)}, u32[]{:S(2)}) collective-permute-start(bf16[128,512]{1,0:T(8,128)(2,1)S(1)} %get-tuple-element.1222), channel_id=1, source_target_pairs={{0,1},{1,2},{2,3},{3,4},{4,5},{5,6},{6,7},{7,8},{8,9},{9,10},{10,1... | collective-permute-start | bytes 393224 | tf_op jit(solution)/shard_map/while/body/eval_jaxpr/ppermute | solution.py:18
  35.2 8.8 %collective-permute-start.1 = (s32[128]{0:T(128)S(1)}, s32[128]{0:T(128)S(1)}, u32[]{:S(2)}, u32[]{:S(2)}) collective-permute-start(s32[128]{0:T(128)S(1)} %get-tuple-element.1223), channel_id=1, source_target_pairs={{0,1},{1,2},{2,3},{3,4},{4,5},{5,6},{6,7},{7,8},{8,9},{9,10},{10,1... | collective-permute-start | bytes 1544 | tf_op jit(solution)/shard_map/while/body/eval_jaxpr/ppermute | solution.py:18
  44.7 10.7 %collective-permute-start = (bf16[128,512]{1,0:T(8,128)(2,1)S(1)}, bf16[128,512]{1,0:T(8,128)(2,1)S(1)}, u32[]{:S(2)}, u32[]{:S(2)}) collective-permute-start(bf16[128,512]{1,0:T(8,128)(2,1)S(1)} %get-tuple-element.1222), channel_id=1, source_target_pairs={{0,1},{1,2},{2,3},{3,4},{4,5},{5,6},{6,7},{7,8},{8,9},{9,10},{10,1... | collective-permute-start | bytes 393224 | tf_op jit(solution)/shard_map/while/body/eval_jaxpr/ppermute | solution.py:18
  46.6 8.8 %collective-permute-start.1 = (s32[128]{0:T(128)S(1)}, s32[128]{0:T(128)S(1)}, u32[]{:S(2)}, u32[]{:S(2)}) collective-permute-start(s32[128]{0:T(128)S(1)} %get-tuple-element.1223), channel_id=1, source_target_pairs={{0,1},{1,2},{2,3},{3,4},{4,5},{5,6},{6,7},{7,8},{8,9},{9,10},{10,1... | collective-permute-start | bytes 1544 | tf_op jit(solution)/shard_map/while/body/eval_jaxpr/ppermute | solution.py:18
  56.0 10.7 %collective-permute-start = (bf16[128,512]{1,0:T(8,128)(2,1)S(1)}, bf16[128,512]{1,0:T(8,128)(2,1)S(1)}, u32[]{:S(2)}, u32[]{:S(2)}) collective-permute-start(bf16[128,512]{1,0:T(8,128)(2,1)S(1)} %get-tuple-element.1222), channel_id=1, source_target_pairs={{0,1},{1,2},{2,3},{3,4},{4,5},{5,6},{6,7},{7,8},{8,9},{9,10},{10,1... | collective-permute-start | bytes 393224 | tf_op jit(solution)/shard_map/while/body/eval_jaxpr/ppermute | solution.py:18
  58.0 8.8 %collective-permute-start.1 = (s32[128]{0:T(128)S(1)}, s32[128]{0:T(128)S(1)}, u32[]{:S(2)}, u32[]{:S(2)}) collective-permute-start(s32[128]{0:T(128)S(1)} %get-tuple-element.1223), channel_id=1, source_target_pairs={{0,1},{1,2},{2,3},{3,4},{4,5},{5,6},{6,7},{7,8},{8,9},{9,10},{10,1... | collective-permute-start | bytes 1544 | tf_op jit(solution)/shard_map/while/body/eval_jaxpr/ppermute | solution.py:18
  67.4 10.7 %collective-permute-start = (bf16[128,512]{1,0:T(8,128)(2,1)S(1)}, bf16[128,512]{1,0:T(8,128)(2,1)S(1)}, u32[]{:S(2)}, u32[]{:S(2)}) collective-permute-start(bf16[128,512]{1,0:T(8,128)(2,1)S(1)} %get-tuple-element.1222), channel_id=1, source_target_pairs={{0,1},{1,2},{2,3},{3,4},{4,5},{5,6},{6,7},{7,8},{8,9},{9,10},{10,1... | collective-permute-start | bytes 393224 | tf_op jit(solution)/shard_map/while/body/eval_jaxpr/ppermute | solution.py:18
  69.3 8.8 %collective-permute-start.1 = (s32[128]{0:T(128)S(1)}, s32[128]{0:T(128)S(1)}, u32[]{:S(2)}, u32[]{:S(2)}) collective-permute-start(s32[128]{0:T(128)S(1)} %get-tuple-element.1223), channel_id=1, source_target_pairs={{0,1},{1,2},{2,3},{3,4},{4,5},{5,6},{6,7},{7,8},{8,9},{9,10},{10,1... | collective-permute-start | bytes 1544 | tf_op jit(solution)/shard_map/while/body/eval_jaxpr/ppermute | solution.py:18
  78.8 10.7 %collective-permute-start = (bf16[128,512]{1,0:T(8,128)(2,1)S(1)}, bf16[128,512]{1,0:T(8,128)(2,1)S(1)}, u32[]{:S(2)}, u32[]{:S(2)}) collective-permute-start(bf16[128,512]{1,0:T(8,128)(2,1)S(1)} %get-tuple-element.1222), channel_id=1, source_target_pairs={{0,1},{1,2},{2,3},{3,4},{4,5},{5,6},{6,7},{7,8},{8,9},{9,10},{10,1... | collective-permute-start | bytes 393224 | tf_op jit(solution)/shard_map/while/body/eval_jaxpr/ppermute | solution.py:18
  80.7 8.8 %collective-permute-start.1 = (s32[128]{0:T(128)S(1)}, s32[128]{0:T(128)S(1)}, u32[]{:S(2)}, u32[]{:S(2)}) collective-permute-start(s32[128]{0:T(128)S(1)} %get-tuple-element.1223), channel_id=1, source_target_pairs={{0,1},{1,2},{2,3},{3,4},{4,5},{5,6},{6,7},{7,8},{8,9},{9,10},{10,1... | collective-permute-start | bytes 1544 | tf_op jit(solution)/shard_map/while/body/eval_jaxpr/ppermute | solution.py:18
  90.2 10.9 %collective-permute-start = (bf16[128,512]{1,0:T(8,128)(2,1)S(1)}, bf16[128,512]{1,0:T(8,128)(2,1)S(1)}, u32[]{:S(2)}, u32[]{:S(2)}) collective-permute-start(bf16[128,512]{1,0:T(8,128)(2,1)S(1)} %get-tuple-element.1222), channel_id=1, source_target_pairs={{0,1},{1,2},{2,3},{3,4},{4,5},{5,6},{6,7},{7,8},{8,9},{9,10},{10,1... | collective-permute-start | bytes 393224 | tf_op jit(solution)/shard_map/while/body/eval_jaxpr/ppermute | solution.py:18
  92.1 9.0 %collective-permute-start.1 = (s32[128]{0:T(128)S(1)}, s32[128]{0:T(128)S(1)}, u32[]{:S(2)}, u32[]{:S(2)}) collective-permute-start(s32[128]{0:T(128)S(1)} %get-tuple-element.1223), channel_id=1, source_target_pairs={{0,1},{1,2},{2,3},{3,4},{4,5},{5,6},{6,7},{7,8},{8,9},{9,10},{10,1... | collective-permute-start | bytes 1544 | tf_op jit(solution)/shard_map/while/body/eval_jaxpr/ppermute | solution.py:18
  101.8 11.3 %collective-permute-start = (bf16[128,512]{1,0:T(8,128)(2,1)S(1)}, bf16[128,512]{1,0:T(8,128)(2,1)S(1)}, u32[]{:S(2)}, u32[]{:S(2)}) collective-permute-start(bf16[128,512]{1,0:T(8,128)(2,1)S(1)} %get-tuple-element.1222), channel_id=1, source_target_pairs={{0,1},{1,2},{2,3},{3,4},{4,5},{5,6},{6,7},{7,8},{8,9},{9,10},{10,1... | collective-permute-start | bytes 393224 | tf_op jit(solution)/shard_map/while/body/eval_jaxpr/ppermute | solution.py:18
  103.7 9.3 %collective-permute-start.1 = (s32[128]{0:T(128)S(1)}, s32[128]{0:T(128)S(1)}, u32[]{:S(2)}, u32[]{:S(2)}) collective-permute-start(s32[128]{0:T(128)S(1)} %get-tuple-element.1223), channel_id=1, source_target_pairs={{0,1},{1,2},{2,3},{3,4},{4,5},{5,6},{6,7},{7,8},{8,9},{9,10},{10,1... | collective-permute-start | bytes 1544 | tf_op jit(solution)/shard_map/while/body/eval_jaxpr/ppermute | solution.py:18
  113.7 10.7 %collective-permute-start = (bf16[128,512]{1,0:T(8,128)(2,1)S(1)}, bf16[128,512]{1,0:T(8,128)(2,1)S(1)}, u32[]{:S(2)}, u32[]{:S(2)}) collective-permute-start(bf16[128,512]{1,0:T(8,128)(2,1)S(1)} %get-tuple-element.1222), channel_id=1, source_target_pairs={{0,1},{1,2},{2,3},{3,4},{4,5},{5,6},{6,7},{7,8},{8,9},{9,10},{10,1... | collective-permute-start | bytes 393224 | tf_op jit(solution)/shard_map/while/body/eval_jaxpr/ppermute | solution.py:18
  115.7 8.8 %collective-permute-start.1 = (s32[128]{0:T(128)S(1)}, s32[128]{0:T(128)S(1)}, u32[]{:S(2)}, u32[]{:S(2)}) collective-permute-start(s32[128]{0:T(128)S(1)} %get-tuple-element.1223), channel_id=1, source_target_pairs={{0,1},{1,2},{2,3},{3,4},{4,5},{5,6},{6,7},{7,8},{8,9},{9,10},{10,1... | collective-permute-start | bytes 1544 | tf_op jit(solution)/shard_map/while/body/eval_jaxpr/ppermute | solution.py:18
  125.1 10.7 %collective-permute-start = (bf16[128,512]{1,0:T(8,128)(2,1)S(1)}, bf16[128,512]{1,0:T(8,128)(2,1)S(1)}, u32[]{:S(2)}, u32[]{:S(2)}) collective-permute-start(bf16[128,512]{1,0:T(8,128)(2,1)S(1)} %get-tuple-element.1222), channel_id=1, source_target_pairs={{0,1},{1,2},{2,3},{3,4},{4,5},{5,6},{6,7},{7,8},{8,9},{9,10},{10,1... | collective-permute-start | bytes 393224 | tf_op jit(solution)/shard_map/while/body/eval_jaxpr/ppermute | solution.py:18
  127.1 8.8 %collective-permute-start.1 = (s32[128]{0:T(128)S(1)}, s32[128]{0:T(128)S(1)}, u32[]{:S(2)}, u32[]{:S(2)}) collective-permute-start(s32[128]{0:T(128)S(1)} %get-tuple-element.1223), channel_id=1, source_target_pairs={{0,1},{1,2},{2,3},{3,4},{4,5},{5,6},{6,7},{7,8},{8,9},{9,10},{10,1... | collective-permute-start | bytes 1544 | tf_op jit(solution)/shard_map/while/body/eval_jaxpr/ppermute | solution.py:18
  136.5 10.7 %collective-permute-start = (bf16[128,512]{1,0:T(8,128)(2,1)S(1)}, bf16[128,512]{1,0:T(8,128)(2,1)S(1)}, u32[]{:S(2)}, u32[]{:S(2)}) collective-permute-start(bf16[128,512]{1,0:T(8,128)(2,1)S(1)} %get-tuple-element.1222), channel_id=1, source_target_pairs={{0,1},{1,2},{2,3},{3,4},{4,5},{5,6},{6,7},{7,8},{8,9},{9,10},{10,1... | collective-permute-start | bytes 393224 | tf_op jit(solution)/shard_map/while/body/eval_jaxpr/ppermute | solution.py:18
  138.4 8.8 %collective-permute-start.1 = (s32[128]{0:T(128)S(1)}, s32[128]{0:T(128)S(1)}, u32[]{:S(2)}, u32[]{:S(2)}) collective-permute-start(s32[128]{0:T(128)S(1)} %get-tuple-element.1223), channel_id=1, source_target_pairs={{0,1},{1,2},{2,3},{3,4},{4,5},{5,6},{6,7},{7,8},{8,9},{9,10},{10,1... | collective-permute-start | bytes 1544 | tf_op jit(solution)/shard_map/while/body/eval_jaxpr/ppermute | solution.py:18
  147.9 10.7 %collective-permute-start = (bf16[128,512]{1,0:T(8,128)(2,1)S(1)}, bf16[128,512]{1,0:T(8,128)(2,1)S(1)}, u32[]{:S(2)}, u32[]{:S(2)}) collective-permute-start(bf16[128,512]{1,0:T(8,128)(2,1)S(1)} %get-tuple-element.1222), channel_id=1, source_target_pairs={{0,1},{1,2},{2,3},{3,4},{4,5},{5,6},{6,7},{7,8},{8,9},{9,10},{10,1... | collective-permute-start | bytes 393224 | tf_op jit(solution)/shard_map/while/body/eval_jaxpr/ppermute | solution.py:18
  149.8 8.8 %collective-permute-start.1 = (s32[128]{0:T(128)S(1)}, s32[128]{0:T(128)S(1)}, u32[]{:S(2)}, u32[]{:S(2)}) collective-permute-start(s32[128]{0:T(128)S(1)} %get-tuple-element.1223), channel_id=1, source_target_pairs={{0,1},{1,2},{2,3},{3,4},{4,5},{5,6},{6,7},{7,8},{8,9},{9,10},{10,1... | collective-permute-start | bytes 1544 | tf_op jit(solution)/shard_map/while/body/eval_jaxpr/ppermute | solution.py:18
  159.3 10.7 %collective-permute-start = (bf16[128,512]{1,0:T(8,128)(2,1)S(1)}, bf16[128,512]{1,0:T(8,128)(2,1)S(1)}, u32[]{:S(2)}, u32[]{:S(2)}) collective-permute-start(bf16[128,512]{1,0:T(8,128)(2,1)S(1)} %get-tuple-element.1222), channel_id=1, source_target_pairs={{0,1},{1,2},{2,3},{3,4},{4,5},{5,6},{6,7},{7,8},{8,9},{9,10},{10,1... | collective-permute-start | bytes 393224 | tf_op jit(solution)/shard_map/while/body/eval_jaxpr/ppermute | solution.py:18
  161.2 8.8 %collective-permute-start.1 = (s32[128]{0:T(128)S(1)}, s32[128]{0:T(128)S(1)}, u32[]{:S(2)}, u32[]{:S(2)}) collective-permute-start(s32[128]{0:T(128)S(1)} %get-tuple-element.1223), channel_id=1, source_target_pairs={{0,1},{1,2},{2,3},{3,4},{4,5},{5,6},{6,7},{7,8},{8,9},{9,10},{10,1... | collective-permute-start | bytes 1544 | tf_op jit(solution)/shard_map/while/body/eval_jaxpr/ppermute | solution.py:18
  170.7 10.7 %collective-permute-start = (bf16[128,512]{1,0:T(8,128)(2,1)S(1)}, bf16[128,512]{1,0:T(8,128)(2,1)S(1)}, u32[]{:S(2)}, u32[]{:S(2)}) collective-permute-start(bf16[128,512]{1,0:T(8,128)(2,1)S(1)} %get-tuple-element.1222), channel_id=1, source_target_pairs={{0,1},{1,2},{2,3},{3,4},{4,5},{5,6},{6,7},{7,8},{8,9},{9,10},{10,1... | collective-permute-start | bytes 393224 | tf_op jit(solution)/shard_map/while/body/eval_jaxpr/ppermute | solution.py:18
  172.6 8.8 %collective-permute-start.1 = (s32[128]{0:T(128)S(1)}, s32[128]{0:T(128)S(1)}, u32[]{:S(2)}, u32[]{:S(2)}) collective-permute-start(s32[128]{0:T(128)S(1)} %get-tuple-element.1223), channel_id=1, source_target_pairs={{0,1},{1,2},{2,3},{3,4},{4,5},{5,6},{6,7},{7,8},{8,9},{9,10},{10,1... | collective-permute-start | bytes 1544 | tf_op jit(solution)/shard_map/while/body/eval_jaxpr/ppermute | solution.py:18
  209.4 0.9 copy-start
  257.8 10.0 %collective-permute-start.2 = (f32[128,512]{1,0:T(8,128)S(1)}, f32[128,512]{1,0:T(8,128)S(1)}, u32[]{:S(2)}, u32[]{:S(2)}) collective-permute-start(f32[128,512]{1,0:T(8,128)S(1)} %get-tuple-element.1333), channel_id=1, source_target_pairs={{1,0},{2,1},{3,2},{4,3},{5,4},{6,5},{7,6},{8,7},{9,8},{10,9},{11,1... | collective-permute-start | bytes 786440 | tf_op jit(solution)/shard_map/while/body/eval_jaxpr/ppermute | solution.py:18
  268.8 9.5 %collective-permute-start.2 = (f32[128,512]{1,0:T(8,128)S(1)}, f32[128,512]{1,0:T(8,128)S(1)}, u32[]{:S(2)}, u32[]{:S(2)}) collective-permute-start(f32[128,512]{1,0:T(8,128)S(1)} %get-tuple-element.1333), channel_id=1, source_target_pairs={{1,0},{2,1},{3,2},{4,3},{5,4},{6,5},{7,6},{8,7},{9,8},{10,9},{11,1... | collective-permute-start | bytes 786440 | tf_op jit(solution)/shard_map/while/body/eval_jaxpr/ppermute | solution.py:18
  279.3 11.9 %collective-permute-start.2 = (f32[128,512]{1,0:T(8,128)S(1)}, f32[128,512]{1,0:T(8,128)S(1)}, u32[]{:S(2)}, u32[]{:S(2)}) collective-permute-start(f32[128,512]{1,0:T(8,128)S(1)} %get-tuple-element.1333), channel_id=1, source_target_pairs={{1,0},{2,1},{3,2},{4,3},{5,4},{6,5},{7,6},{8,7},{9,8},{10,9},{11,1... | collective-permute-start | bytes 786440 | tf_op jit(solution)/shard_map/while/body/eval_jaxpr/ppermute | solution.py:18
  292.2 13.2 %collective-permute-start.2 = (f32[128,512]{1,0:T(8,128)S(1)}, f32[128,512]{1,0:T(8,128)S(1)}, u32[]{:S(2)}, u32[]{:S(2)}) collective-permute-start(f32[128,512]{1,0:T(8,128)S(1)} %get-tuple-element.1333), channel_id=1, source_target_pairs={{1,0},{2,1},{3,2},{4,3},{5,4},{6,5},{7,6},{8,7},{9,8},{10,9},{11,1... | collective-permute-start | bytes 786440 | tf_op jit(solution)/shard_map/while/body/eval_jaxpr/ppermute | solution.py:18
  306.5 14.4 %collective-permute-start.2 = (f32[128,512]{1,0:T(8,128)S(1)}, f32[128,512]{1,0:T(8,128)S(1)}, u32[]{:S(2)}, u32[]{:S(2)}) collective-permute-start(f32[128,512]{1,0:T(8,128)S(1)} %get-tuple-element.1333), channel_id=1, source_target_pairs={{1,0},{2,1},{3,2},{4,3},{5,4},{6,5},{7,6},{8,7},{9,8},{10,9},{11,1... | collective-permute-start | bytes 786440 | tf_op jit(solution)/shard_map/while/body/eval_jaxpr/ppermute | solution.py:18
  321.8 13.5 %collective-permute-start.2 = (f32[128,512]{1,0:T(8,128)S(1)}, f32[128,512]{1,0:T(8,128)S(1)}, u32[]{:S(2)}, u32[]{:S(2)}) collective-permute-start(f32[128,512]{1,0:T(8,128)S(1)} %get-tuple-element.1333), channel_id=1, source_target_pairs={{1,0},{2,1},{3,2},{4,3},{5,4},{6,5},{7,6},{8,7},{9,8},{10,9},{11,1... | collective-permute-start | bytes 786440 | tf_op jit(solution)/shard_map/while/body/eval_jaxpr/ppermute | solution.py:18
  336.3 12.7 %collective-permute-start.2 = (f32[128,512]{1,0:T(8,128)S(1)}, f32[128,512]{1,0:T(8,128)S(1)}, u32[]{:S(2)}, u32[]{:S(2)}) collective-permute-start(f32[128,512]{1,0:T(8,128)S(1)} %get-tuple-element.1333), channel_id=1, source_target_pairs={{1,0},{2,1},{3,2},{4,3},{5,4},{6,5},{7,6},{8,7},{9,8},{10,9},{11,1... | collective-permute-start | bytes 786440 | tf_op jit(solution)/shard_map/while/body/eval_jaxpr/ppermute | solution.py:18
  350.1 11.8 %collective-permute-start.2 = (f32[128,512]{1,0:T(8,128)S(1)}, f32[128,512]{1,0:T(8,128)S(1)}, u32[]{:S(2)}, u32[]{:S(2)}) collective-permute-start(f32[128,512]{1,0:T(8,128)S(1)} %get-tuple-element.1333), channel_id=1, source_target_pairs={{1,0},{2,1},{3,2},{4,3},{5,4},{6,5},{7,6},{8,7},{9,8},{10,9},{11,1... | collective-permute-start | bytes 786440 | tf_op jit(solution)/shard_map/while/body/eval_jaxpr/ppermute | solution.py:18
  362.8 11.6 %collective-permute-start.2 = (f32[128,512]{1,0:T(8,128)S(1)}, f32[128,512]{1,0:T(8,128)S(1)}, u32[]{:S(2)}, u32[]{:S(2)}) collective-permute-start(f32[128,512]{1,0:T(8,128)S(1)} %get-tuple-element.1333), channel_id=1, source_target_pairs={{1,0},{2,1},{3,2},{4,3},{5,4},{6,5},{7,6},{8,7},{9,8},{10,9},{11,1... | collective-permute-start | bytes 786440 | tf_op jit(solution)/shard_map/while/body/eval_jaxpr/ppermute | solution.py:18
  375.4 11.6 %collective-permute-start.2 = (f32[128,512]{1,0:T(8,128)S(1)}, f32[128,512]{1,0:T(8,128)S(1)}, u32[]{:S(2)}, u32[]{:S(2)}) collective-permute-start(f32[128,512]{1,0:T(8,128)S(1)} %get-tuple-element.1333), channel_id=1, source_target_pairs={{1,0},{2,1},{3,2},{4,3},{5,4},{6,5},{7,6},{8,7},{9,8},{10,9},{11,1... | collective-permute-start | bytes 786440 | tf_op jit(solution)/shard_map/while/body/eval_jaxpr/ppermute | solution.py:18
  388.0 11.6 %collective-permute-start.2 = (f32[128,512]{1,0:T(8,128)S(1)}, f32[128,512]{1,0:T(8,128)S(1)}, u32[]{:S(2)}, u32[]{:S(2)}) collective-permute-start(f32[128,512]{1,0:T(8,128)S(1)} %get-tuple-element.1333), channel_id=1, source_target_pairs={{1,0},{2,1},{3,2},{4,3},{5,4},{6,5},{7,6},{8,7},{9,8},{10,9},{11,1... | collective-permute-start | bytes 786440 | tf_op jit(solution)/shard_map/while/body/eval_jaxpr/ppermute | solution.py:18
  400.6 11.6 %collective-permute-start.2 = (f32[128,512]{1,0:T(8,128)S(1)}, f32[128,512]{1,0:T(8,128)S(1)}, u32[]{:S(2)}, u32[]{:S(2)}) collective-permute-start(f32[128,512]{1,0:T(8,128)S(1)} %get-tuple-element.1333), channel_id=1, source_target_pairs={{1,0},{2,1},{3,2},{4,3},{5,4},{6,5},{7,6},{8,7},{9,8},{10,9},{11,1... | collective-permute-start | bytes 786440 | tf_op jit(solution)/shard_map/while/body/eval_jaxpr/ppermute | solution.py:18
  413.2 11.6 %collective-permute-start.2 = (f32[128,512]{1,0:T(8,128)S(1)}, f32[128,512]{1,0:T(8,128)S(1)}, u32[]{:S(2)}, u32[]{:S(2)}) collective-permute-start(f32[128,512]{1,0:T(8,128)S(1)} %get-tuple-element.1333), channel_id=1, source_target_pairs={{1,0},{2,1},{3,2},{4,3},{5,4},{6,5},{7,6},{8,7},{9,8},{10,9},{11,1... | collective-permute-start | bytes 786440 | tf_op jit(solution)/shard_map/while/body/eval_jaxpr/ppermute | solution.py:18
  425.8 11.6 %collective-permute-start.2 = (f32[128,512]{1,0:T(8,128)S(1)}, f32[128,512]{1,0:T(8,128)S(1)}, u32[]{:S(2)}, u32[]{:S(2)}) collective-permute-start(f32[128,512]{1,0:T(8,128)S(1)} %get-tuple-element.1333), channel_id=1, source_target_pairs={{1,0},{2,1},{3,2},{4,3},{5,4},{6,5},{7,6},{8,7},{9,8},{10,9},{11,1... | collective-permute-start | bytes 786440 | tf_op jit(solution)/shard_map/while/body/eval_jaxpr/ppermute | solution.py:18
  438.4 11.6 %collective-permute-start.2 = (f32[128,512]{1,0:T(8,128)S(1)}, f32[128,512]{1,0:T(8,128)S(1)}, u32[]{:S(2)}, u32[]{:S(2)}) collective-permute-start(f32[128,512]{1,0:T(8,128)S(1)} %get-tuple-element.1333), channel_id=1, source_target_pairs={{1,0},{2,1},{3,2},{4,3},{5,4},{6,5},{7,6},{8,7},{9,8},{10,9},{11,1... | collective-permute-start | bytes 786440 | tf_op jit(solution)/shard_map/while/body/eval_jaxpr/ppermute | solution.py:18
